TPU v7x, 32 devices: a whole 2x2x4 slice. The times are simulated.
32 devices in a mesh: ctx: 4 (over y, core), tp: 4 (over z), dp: 2 (over x).
Axes of the slice: x: 2, y: 2, z: 4, core: 2. Of those that a mesh axis runs over, the one named last changes fastest.
Arguments:
- tokens: bfloat16 [3072, 3584], P(('dp', 'ctx'), 'tp'), may hold values from -6 to 6
- expert_ids: int32 [3072, 8], P(('dp', 'ctx')), may hold values from 0 to 255, all different within a row; in each aligned block of 384 rows (0 to 383, 384 to 767, ...) at most 24 rows name the same one
- gate_codes: int32 [3072, 8], P(('dp', 'ctx')), may hold values from 1 to 32767
- up_weight: bfloat16 [4, 3584, 1024], P('ctx', 'tp', 'dp'), may hold values from -0.09375 to 0.09375
- down_weight: bfloat16 [4, 1024, 3584], P('ctx', 'dp', 'tp'), may hold values from -0.1875 to 0.1875
- cotangent: bfloat16 [3072, 3584], P(('dp', 'ctx'), 'tp'), may hold values from -6 to 6
Outputs:
- mixed: bfloat16 [3072, 3584], P(('dp', 'ctx'), 'tp')
- grad_tokens: bfloat16 [3072, 3584], P(('dp', 'ctx'), 'tp')
- grad_up: bfloat16 [4, 3584, 1024], P('ctx', 'tp', 'dp')
- grad_down: bfloat16 [4, 1024, 3584], P('ctx', 'dp', 'tp')
Inputs may be any that keep to these rules, and one draw needn't show every extreme that they name: `expert_ids`: each row names 8 different experts; among the 384 rows of one device no expert is named more than 24 times.
All inputs are finite; a program needn't handle non-finite values.
Results may differ from a plain program's by a relative error of at most 0.0066.
Values may be sent and summed in bfloat16 or wider, within the bound.
A program may use at most 64 MiB of HBM per device.

v0:
```python
import jax
import jax.numpy as jnp
from jax import lax
from jax.sharding import PartitionSpec as P


def place_slots(expert_ids, gate_codes, experts, capacity):
    rows_count, picks = expert_ids.shape
    flat_ids = expert_ids.reshape(-1)
    one_hot = (flat_ids[:, None] == jnp.arange(experts, dtype=jnp.int32)[None, :]).astype(jnp.int32)
    before = jnp.cumsum(one_hot, axis=0) - one_hot
    slot_rank = jnp.sum(before * one_hot, axis=1)
    inside = flat_ids < experts
    target = jnp.where(inside, flat_ids * capacity + slot_rank, experts * capacity)
    source = jnp.arange(rows_count * picks, dtype=jnp.int32) // picks
    slot_token = (
        jnp.full((experts * capacity,), rows_count, jnp.int32).at[target].set(source, mode="drop")
    )
    weights = gate_codes.reshape(-1).astype(jnp.float32) / 32768.0
    gate_slot = jnp.zeros((experts * capacity,), jnp.float32).at[target].set(weights, mode="drop")
    return (slot_token, gate_slot)


def silu_grad(values):
    sigma = jax.nn.sigmoid(values)
    return sigma * (1.0 + values * (1.0 - sigma))


def body(tokens, expert_ids, gate_codes, up_weight, down_weight, cotangent):
    sources = lax.axis_size("ctx")
    rows_count, features = tokens.shape
    capacity = rows_count // 16
    slot_token, gate_slot = place_slots(expert_ids, gate_codes, sources, capacity)
    padded_x = jnp.concatenate([tokens, jnp.zeros((1, features), tokens.dtype)], axis=0)
    outgoing = padded_x[slot_token].reshape(sources, capacity, features)
    arrived = lax.all_to_all(outgoing, "ctx", split_axis=0, concat_axis=0, tiled=True).reshape(
        sources * capacity, features
    )
    w_up, w_down = (
        lax.all_gather(up_weight[0], "dp", axis=1, tiled=True),
        lax.all_gather(down_weight[0], "dp", axis=0, tiled=True),
    )
    hidden = lax.psum(jnp.dot(arrived, w_up, preferred_element_type=jnp.float32), "tp")
    active = jax.nn.silu(hidden).astype(jnp.bfloat16)
    produced = jnp.dot(active, w_down, preferred_element_type=jnp.float32).astype(jnp.bfloat16)
    returned = lax.all_to_all(
        produced.reshape(sources, capacity, features),
        "ctx",
        split_axis=0,
        concat_axis=0,
        tiled=True,
    ).reshape(sources * capacity, features)
    mixed = (
        jnp.zeros((rows_count + 1, features), jnp.float32)
        .at[slot_token]
        .add(gate_slot[:, None] * returned.astype(jnp.float32))
    )
    mixed = mixed[:rows_count].astype(jnp.bfloat16)
    padded_c = jnp.concatenate([cotangent, jnp.zeros((1, features), cotangent.dtype)], axis=0)
    grad_send = (gate_slot[:, None] * padded_c[slot_token].astype(jnp.float32)).astype(jnp.bfloat16)
    grad_rows = lax.all_to_all(
        grad_send.reshape(sources, capacity, features),
        "ctx",
        split_axis=0,
        concat_axis=0,
        tiled=True,
    ).reshape(sources * capacity, features)
    contract_last = (((1,), (1,)), ((), ()))
    contract_first = (((0,), (0,)), ((), ()))
    grad_act = lax.psum(
        lax.dot_general(grad_rows, w_down, contract_last, preferred_element_type=jnp.float32), "tp"
    )
    grad_hid = (grad_act * silu_grad(hidden)).astype(jnp.bfloat16)
    grad_in = lax.dot_general(
        grad_hid, w_up, contract_last, preferred_element_type=jnp.float32
    ).astype(jnp.bfloat16)
    back_rows = lax.all_to_all(
        grad_in.reshape(sources, capacity, features), "ctx", split_axis=0, concat_axis=0, tiled=True
    ).reshape(sources * capacity, features)
    grad_tokens = (
        jnp.zeros((rows_count + 1, features), jnp.float32)
        .at[slot_token]
        .add(back_rows.astype(jnp.float32))
    )
    grad_tokens = grad_tokens[:rows_count].astype(jnp.bfloat16)
    part_up = lax.dot_general(arrived, grad_hid, contract_first, preferred_element_type=jnp.float32)
    part_down = lax.dot_general(
        active, grad_rows, contract_first, preferred_element_type=jnp.float32
    )
    grad_up, grad_down = (
        lax.psum_scatter(
            part_up.astype(jnp.bfloat16), "dp", scatter_dimension=1, tiled=True
        ).astype(jnp.float32),
        lax.psum_scatter(
            part_down.astype(jnp.bfloat16), "dp", scatter_dimension=0, tiled=True
        ).astype(jnp.float32),
    )
    return (
        mixed,
        grad_tokens,
        grad_up.astype(jnp.bfloat16)[None],
        grad_down.astype(jnp.bfloat16)[None],
    )


def solution(mesh):
    return jax.shard_map(
        body,
        mesh=mesh,
        in_specs=(
            P(("dp", "ctx"), "tp"),
            P(("dp", "ctx"), None),
            P(("dp", "ctx"), None),
            P("ctx", "tp", "dp"),
            P("ctx", "dp", "tp"),
            P(("dp", "ctx"), "tp"),
        ),
        out_specs=(
            P(("dp", "ctx"), "tp"),
            P(("dp", "ctx"), "tp"),
            P("ctx", "tp", "dp"),
            P("ctx", "dp", "tp"),
        ),
        check_vma=False,
    )
```

profile of v0, /device:TPU:0, one launch (start us, length us, event | category | flops | bytes accessed | tf_op | source)
XLA Modules:
  0.0 190.8 jit_solution(14327130908680088390)
XLA Ops:
  7.2 0.7 all-gather.5.cloned.1.call-update
  8.0 0.7 all-gather.7.cloned.1.call-update
  9.1 0.2 copy.10
  9.7 1.2 reduce-window.6
  10.9 0.2 slice_reduce_fusion
  11.1 0.2 reduce-window.9
  11.6 11.8 %scatter_custom_fusion = s32[96]{0:T(128)S(1)} fusion(s32[3072]{0:T(1024)S(1)} %bitcast.64, s32[3072]{0:T(1024)S(1)} %add_select_fusion, s32[]{:T(128)} %constant.17.clone.1), kind=kCustom, calls=%fused_computation.56 | custom fusion | bytes 388 | tf_op jit(solution)/shard_map/scatter | solution.py:17
  23.4 1.5 gather_fusion
  24.9 4.3 %all-to-all-start = ((bf16[4,24,896]{2,1,0:T(8,128)(2,1)}), bf16[4,24,896]{2,1,0:T(8,128)(2,1)S(1)}, u32[]{:S(2)}, u32[]{:S(2)}) async-start(bf16[4,24,896]{2,1,0:T(8,128)(2,1)} %bitcast.3), calls=%async_computation | async-start | bytes 344064 | tf_op jit(solution)/shard_map/all_to_all | solution.py:36
  29.4 11.8 %scatter_custom_fusion.1 = f32[96]{0:T(128)S(1)} fusion(s32[3072]{0:T(1024)S(1)} %bitcast.65, f32[3072]{0:T(1024)S(1)} %reshape.139, f32[]{:T(128)} %constant.15.clone.1), kind=kCustom, calls=%fused_computation.54 | custom fusion | bytes 388 | tf_op jit(solution)/shard_map/scatter | solution.py:20
  41.3 0.8 gather_fusion.1
  42.1 0.8 fusion.19
  42.9 3.4 %all-to-all-start.2 = ((bf16[4,24,896]{2,1,0:T(8,128)(2,1)}), bf16[4,24,896]{2,1,0:T(8,128)(2,1)S(1)}, u32[]{:S(2)}, u32[]{:S(2)}) async-start(bf16[4,24,896]{2,1,0:T(8,128)(2,1)} %fusion.19), calls=%async_computation.2 | async-start | bytes 344064 | tf_op jit(solution)/shard_map/all_to_all | solution.py:61
  46.3 2.7 %fusion.6 = f32[96,1024]{1,0:T(8,128)} fusion(bf16[96,896]{1,0:T(8,128)(2,1)S(1)} %bitcast.56, bf16[1,896,1024]{2,1,0:T(8,128)(2,1)} %all-gather.5.cloned.1.call-done), kind=kOutput, calls=%fused_computation.12 | convolution fusion | flops 176160768 | bytes 2400256 | tf_op jit(solution)/shard_map/dot_general | solution.py:43
  49.0 2.3 %all-to-all-done.2 = bf16[4,24,896]{2,1,0:T(8,128)(2,1)S(1)} async-done(((bf16[4,24,896]{2,1,0:T(8,128)(2,1)}), bf16[4,24,896]{2,1,0:T(8,128)(2,1)S(1)}, u32[]{:S(2)}, u32[]{:S(2)}) %all-to-all-start.2) | async-done | bytes 172064 | tf_op jit(solution)/shard_map/all_to_all | solution.py:61
  51.3 22.8 %all-gather.7.cloned.1.call-done = bf16[1,1024,896]{2,1,0:T(8,128)(2,1)} async-done(((bf16[1,512,896]{2,1,0:T(8,128)(2,1)}), bf16[1,1024,896]{2,1,0:T(8,128)(2,1)}) %all-gather.7.cloned.1.call-update) | async-done | bytes 1835024 | tf_op jit(solution)/shard_map/all_gather | solution.py:41
  74.1 2.9 %fusion = f32[96,1024]{1,0:T(8,128)} fusion(bf16[96,896]{1,0:T(8,128)(2,1)S(1)} %bitcast.58, bf16[1,1024,896]{2,1,0:T(8,128)(2,1)} %all-gather.7.cloned.1.call-done), kind=kOutput, calls=%fused_computation.6 | convolution fusion | flops 176160768 | bytes 2400256 | tf_op jit(solution)/shard_map/dot_general | solution.py:71
  77.2 44.0 %all-reduce.5.cloned.1.call-done = (f32[96,1024]{1,0:T(8,128)}, f32[96,1024]{1,0:T(8,128)}) async-done(((f32[96,1024]{1,0:T(8,128)}, f32[96,1024]{1,0:T(8,128)}), (f32[96,1024]{1,0:T(8,128)}, f32[96,1024]{1,0:T(8,128)})) %all-reduce.5.cloned.1.call-update) | async-done | bytes 786448 | tf_op jit(solution)/shard_map/psum | solution.py:43
  121.2 3.0 %convolution_convert_fusion = bf16[1024,896]{1,0:T(8,128)(2,1)} fusion(bf16[96,896]{1,0:T(8,128)(2,1)S(1)} %bitcast.59, f32[96,1024]{1,0:T(8,128)} %get-tuple-element.4), kind=kOutput, calls=%fused_computation.14 | convolution fusion | flops 177569792 | bytes 2400256 | tf_op jit(solution)/shard_map/dot_general | solution.py:87
  124.4 1.9 %convolution_convert_fusion.1 = bf16[896,1024]{1,0:T(8,128)(2,1)} fusion(bf16[96,896]{1,0:T(8,128)(2,1)S(1)} %bitcast.57, bf16[96,1024]{1,0:T(8,128)(2,1)S(1)} %multiply_convert_fusion), kind=kOutput, calls=%fused_computation.15 | convolution fusion | flops 177078272 | bytes 2203648 | tf_op jit(solution)/shard_map/dot_general | solution.py:86
  126.4 2.8 %fusion.11 = bf16[96,896]{1,0:T(8,128)(2,1)} fusion(bf16[1,1024,896]{2,1,0:T(8,128)(2,1)} %all-gather.7.cloned.1.call-done, f32[96,1024]{1,0:T(8,128)S(1)} %copy-done.1), kind=kOutput, calls=%fused_computation.19 | convolution fusion | flops 176738304 | bytes 2400256 | tf_op jit(solution)/shard_map/dot_general | solution.py:45
  129.1 3.4 %all-to-all-start.1 = ((bf16[4,24,896]{2,1,0:T(8,128)(2,1)}), bf16[4,24,896]{2,1,0:T(8,128)(2,1)S(1)}, u32[]{:S(2)}, u32[]{:S(2)}) async-start(bf16[4,24,896]{2,1,0:T(8,128)(2,1)} %bitcast.7), calls=%async_computation.1 | async-start | bytes 344064 | tf_op jit(solution)/shard_map/all_to_all | solution.py:46
  132.5 1.3 fusion.8
  133.8 3.7 %all-to-all-done.1 = bf16[4,24,896]{2,1,0:T(8,128)(2,1)S(1)} async-done(((bf16[4,24,896]{2,1,0:T(8,128)(2,1)}), bf16[4,24,896]{2,1,0:T(8,128)(2,1)S(1)}, u32[]{:S(2)}, u32[]{:S(2)}) %all-to-all-start.1) | async-done | bytes 172064 | tf_op jit(solution)/shard_map/all_to_all | solution.py:46
  137.5 3.3 %all-to-all-start.3 = ((bf16[4,24,896]{2,1,0:T(8,128)(2,1)}), bf16[4,24,896]{2,1,0:T(8,128)(2,1)S(1)}, u32[]{:S(2)}, u32[]{:S(2)}) async-start(bf16[4,24,896]{2,1,0:T(8,128)(2,1)} %bitcast.11), calls=%async_computation.3 | async-start | bytes 344064 | tf_op jit(solution)/shard_map/all_to_all | solution.py:77
  140.8 1.8 scatter_custom_fusion.2
  142.6 0.9 slice.29
  143.6 2.3 %all-to-all-done.3 = bf16[4,24,896]{2,1,0:T(8,128)(2,1)S(1)} async-done(((bf16[4,24,896]{2,1,0:T(8,128)(2,1)}), bf16[4,24,896]{2,1,0:T(8,128)(2,1)S(1)}, u32[]{:S(2)}, u32[]{:S(2)}) %all-to-all-start.3) | async-done | bytes 172064 | tf_op jit(solution)/shard_map/all_to_all | solution.py:77
  145.9 1.7 scatter_custom_fusion.3
  147.6 0.9 slice.28
  148.5 4.1 %reduce-scatter.5.cloned.1.call-done = bf16[512,896]{1,0:T(8,128)(2,1)} async-done(((bf16[1024,896]{1,0:T(8,128)(2,1)}), bf16[512,896]{1,0:T(8,128)(2,1)}) %reduce-scatter.5.cloned.1.call-update) | async-done | bytes 917520 | tf_op jit(solution)/shard_map/reduce_scatter | solution.py:94
  152.5 31.7 %reduce-scatter.3.cloned.1.call-done = bf16[896,512]{1,0:T(8,128)(2,1)} async-done(((bf16[896,1024]{1,0:T(8,128)(2,1)}), bf16[896,512]{1,0:T(8,128)(2,1)}) %reduce-scatter.3.cloned.1.call-update) | async-done | bytes 917520 | tf_op jit(solution)/shard_map/reduce_scatter | solution.py:91
  (46 shorter events, 1.9 us)
Async XLA Ops:
  7.2 1.5 copy-start.5
  7.2 4.3 %copy-start.2 = (bf16[384,896]{1,0:T(8,128)(2,1)S(1)}, bf16[384,896]{1,0:T(8,128)(2,1)}, u32[]{:S(2)}) copy-start(bf16[384,896]{1,0:T(8,128)(2,1)} %param.6) | copy-start | bytes 2064388
  7.2 39.1 %all-gather.5.cloned.1.call-start = ((), (), s32[]{:S(2)}) async-start(), calls=%async_computation.8 | async-start | bytes 2752512 | tf_op jit(solution)/shard_map/all_gather | solution.py:40
  7.9 66.2 %all-gather.7.cloned.1.call-start = ((), (), s32[]{:S(2)}) async-start(), calls=%async_computation.9 | async-start | bytes 2752512 | tf_op jit(solution)/shard_map/all_gather | solution.py:41
  9.7 19.4 %copy-start.6 = (s32[384,8]{0,1:T(8,128)S(1)}, s32[384,8]{0,1:T(8,128)}, u32[]{:S(2)}) copy-start(s32[384,8]{0,1:T(8,128)} %param.8) | copy-start | bytes 36868
  11.5 29.8 %copy-start.3 = (bf16[384,896]{1,0:T(8,128)(2,1)S(1)}, bf16[384,896]{1,0:T(8,128)(2,1)}, u32[]{:S(2)}) copy-start(bf16[384,896]{1,0:T(8,128)(2,1)} %param.11) | copy-start | bytes 2064388
  24.9 18.0 %all-to-all-start = ((bf16[4,24,896]{2,1,0:T(8,128)(2,1)}), bf16[4,24,896]{2,1,0:T(8,128)(2,1)S(1)}, u32[]{:S(2)}, u32[]{:S(2)}) async-start(bf16[4,24,896]{2,1,0:T(8,128)(2,1)} %bitcast.3), calls=%async_computation | async-start | bytes 344064 | tf_op jit(solution)/shard_map/all_to_all | solution.py:36
  42.9 8.4 %all-to-all-start.2 = ((bf16[4,24,896]{2,1,0:T(8,128)(2,1)}), bf16[4,24,896]{2,1,0:T(8,128)(2,1)S(1)}, u32[]{:S(2)}, u32[]{:S(2)}) async-start(bf16[4,24,896]{2,1,0:T(8,128)(2,1)} %fusion.19), calls=%async_computation.2 | async-start | bytes 344064 | tf_op jit(solution)/shard_map/all_to_all | solution.py:61
  46.3 74.9 %all-reduce.5.cloned.1.call-start = ((), (), s32[]{:S(2)}) async-start(), calls=%async_computation.10 | async-start | bytes 1572864 | tf_op jit(solution)/shard_map/psum | solution.py:43
  77.1 75.4 %reduce-scatter.5.cloned.1.call-start = ((), (), s32[]{:S(2)}) async-start(), calls=%async_computation.7 | async-start | bytes 2752512 | tf_op jit(solution)/shard_map/reduce_scatter | solution.py:94
  121.2 3.1 %copy-start.1 = (f32[96,1024]{1,0:T(8,128)S(1)}, f32[96,1024]{1,0:T(8,128)}, u32[]{:S(2)}) copy-start(f32[96,1024]{1,0:T(8,128)} %get-tuple-element.4) | copy-start | bytes 1179652
  121.2 3.1 %copy-start.4 = (f32[96,1024]{1,0:T(8,128)S(1)}, f32[96,1024]{1,0:T(8,128)}, u32[]{:S(2)}) copy-start(f32[96,1024]{1,0:T(8,128)} %get-tuple-element.5) | copy-start | bytes 1179652
  124.2 60.1 %reduce-scatter.3.cloned.1.call-start = ((), (), s32[]{:S(2)}) async-start(), calls=%async_computation.6 | async-start | bytes 2752512 | tf_op jit(solution)/shard_map/reduce_scatter | solution.py:91
  126.4 6.1 %copy-start = (bf16[1,896,1024]{2,1,0:T(8,128)(2,1)S(1)}, bf16[1,896,1024]{2,1,0:T(8,128)(2,1)}, u32[]{:S(2)}) copy-start(bf16[1,896,1024]{2,1,0:T(8,128)(2,1)} %all-gather.5.cloned.1.call-done) | copy-start | bytes 5505028
  129.1 8.4 %all-to-all-start.1 = ((bf16[4,24,896]{2,1,0:T(8,128)(2,1)}), bf16[4,24,896]{2,1,0:T(8,128)(2,1)S(1)}, u32[]{:S(2)}, u32[]{:S(2)}) async-start(bf16[4,24,896]{2,1,0:T(8,128)(2,1)} %bitcast.7), calls=%async_computation.1 | async-start | bytes 344064 | tf_op jit(solution)/shard_map/all_to_all | solution.py:46
  137.5 8.4 %all-to-all-start.3 = ((bf16[4,24,896]{2,1,0:T(8,128)(2,1)}), bf16[4,24,896]{2,1,0:T(8,128)(2,1)S(1)}, u32[]{:S(2)}, u32[]{:S(2)}) async-start(bf16[4,24,896]{2,1,0:T(8,128)(2,1)} %bitcast.11), calls=%async_computation.3 | async-start | bytes 344064 | tf_op jit(solution)/shard_map/all_to_all | solution.py:77
Sparse Core Ops, SparseCore 0:
  9.5 32.8 all-gather.4
  44.0 30.1 all-gather.6
  77.2 43.8 all-reduce.4
  124.3 28.2 reduce-scatter.4
  155.2 29.0 reduce-scatter.2
where the time goes:
time: 191 us
  waiting for transfers between devices  112 us (59%)
  local copies, waits for them, and re-layouts  29.3 us (15%)
  matrix products  14.6 us (8%)
  starting transfers between devices  14.5 us (8%)
  between operations  14.1 us (7%)
  other arithmetic  5.97 us (3%)
    psum x1, waiting for transfers between devices, body(): lax.psum(jnp.dot(arrived, w_up, preferred_element_type=jnp.float32), 'tp')  44 us
    reduce_scatter x1, waiting for transfers between devices, body(): lax.psum_scatter(part_up.astype(jnp.bfloat16), 'dp', scatter_dimension=1,...  31.7 us
    all_gather x1, waiting for transfers between devices, body(): lax.all_gather(down_weight[0], 'dp', axis=0, tiled=True)  22.8 us
    scatter x1, local copies, waits for them, and re-layouts, place_slots(): jnp.full((experts * capacity,), rows_count, jnp.int32).at[target]  11.8 us
    scatter x1, local copies, waits for them, and re-layouts, place_slots(): jnp.zeros((experts * capacity,), jnp.float32).at[target]  11.8 us
    all_to_all x1, starting transfers between devices, body(): lax.all_to_all(outgoing, 'ctx', split_axis=0, concat_axis=0, tiled=True)  4.26 us
    reduce_scatter x1, waiting for transfers between devices, body(): lax.psum_scatter(part_down.astype(jnp.bfloat16), 'dp', scatter_dimension=...  4.05 us
  transfers between devices with their start and end apart: 9, of which 7 were waited for; matrix products, arithmetic and copies ran while one was open for 23% of the time, Pallas kernels for 0%

commit v1 on v0

--- a/solution.py
+++ b/solution.py
@@ -2,6 +2,18 @@
 import jax.numpy as jnp
 from jax import lax
 from jax.sharding import PartitionSpec as P
+
+
+def gather_by_bits(x, axis, dim):
+    ways, here = (lax.axis_size(axis), lax.axis_index(axis))
+    grown, reach = (x, 1)
+    while reach < ways:
+        theirs = lax.ppermute(grown, axis, [(d, d ^ reach) for d in range(ways)])
+        mine_first = jnp.concatenate([grown, theirs], axis=dim)
+        theirs_first = jnp.concatenate([theirs, grown], axis=dim)
+        grown = jnp.where(here & reach == 0, mine_first, theirs_first)
+        reach = 2 * reach
+    return grown
 
 
 def place_slots(expert_ids, gate_codes, experts, capacity):
@@ -38,7 +50,7 @@
     )
     w_up, w_down = (
         lax.all_gather(up_weight[0], "dp", axis=1, tiled=True),
-        lax.all_gather(down_weight[0], "dp", axis=0, tiled=True),
+        gather_by_bits(down_weight[0], "dp", 0),
     )
     hidden = lax.psum(jnp.dot(arrived, w_up, preferred_element_type=jnp.float32), "tp")
     active = jax.nn.silu(hidden).astype(jnp.bfloat16)

time: 191 us -> 175 us (0.916)
  waiting for transfers between devices: 112 us -> 91 us
  starting transfers between devices: 14.5 us -> 16.7 us
    all_gather x1 -> x0, waiting for transfers between devices: 22.8 us -> none  [body(): lax.all_gather(down_weight[0], 'dp', axis=0, tiled=True)]
    ppermute x0 -> x1, starting transfers between devices: none -> 3.03 us  [gather_by_bits(): theirs = lax.ppermute(grown, axis, [(d, d ^ reach) for d in range(ways)])]
    all_to_all x1, waiting for transfers between devices: 0.01 us -> 1.93 us  [body(): lax.all_to_all(outgoing, 'ctx', split_axis=0, concat_axis=0, tiled=True)]
  transfers between devices with their start and end apart: 9 -> 9, of which waited for: 7 -> 7; matrix products, arithmetic and copies ran while one was open for 23% -> 27% of each run, Pallas kernels for 0% -> 0%
where the time goes in v1:
time: 175 us; the launch traced here: 174 us
  waiting for transfers between devices  91 us (52%)
  local copies, waits for them, and re-layouts  30 us (17%)
  starting transfers between devices  16.7 us (10%)
  matrix products  14.9 us (9%)
  between operations  14 us (8%)
  other arithmetic  7.38 us (4%)
    psum x1, waiting for transfers between devices, body(): lax.psum(jnp.dot(arrived, w_up, preferred_element_type=jnp.float32), 'tp')  43.3 us
    reduce_scatter x1, waiting for transfers between devices, body(): lax.psum_scatter(part_up.astype(jnp.bfloat16), 'dp', scatter_dimension=1,...  31.7 us
    scatter x1, local copies, waits for them, and re-layouts, place_slots(): jnp.zeros((experts * capacity,), jnp.float32).at[target]  11.8 us
    scatter x1, local copies, waits for them, and re-layouts, place_slots(): jnp.full((experts * capacity,), rows_count, jnp.int32).at[target]  11.8 us
    reduce_scatter x1, waiting for transfers between devices, body(): lax.psum_scatter(part_down.astype(jnp.bfloat16), 'dp', scatter_dimension=...  3.88 us
    all_to_all x1, waiting for transfers between devices, body(): lax.all_to_all(produced.reshape(sources, capacity, features), 'ctx', spli...  3.65 us
  transfers between devices with their start and end apart: 9, of which 7 were waited for; matrix products, arithmetic and copies ran while one was open for 27% of the time, Pallas kernels for 0%

profile of v1, /device:TPU:0, one launch (start us, length us, event | category | flops | bytes accessed | tf_op | source)
XLA Modules:
  0.0 174.1 jit_solution(3136138067605252014)
XLA Ops:
  7.2 0.7 all-gather.3.cloned.1.call-update
  7.9 3.0 %collective-permute-start = (bf16[512,896]{1,0:T(8,128)(2,1)}, bf16[512,896]{1,0:T(8,128)(2,1)}, u32[]{:S(2)}, u32[]{:S(2)}) collective-permute-start(bf16[512,896]{1,0:T(8,128)(2,1)} %bitcast.61), channel_id=1, source_target_pairs={{0,1},{1,0},{2,3},{3,2},{4,5},{5,4},{6,7},{7,6},{8,9},{9,8},{10,11... | collective-permute-start | bytes 2752520 | tf_op jit(solution)/shard_map/ppermute | solution.py:11
  11.0 0.7 broadcast_compare_fusion
  11.7 0.7 broadcast_multiply_fusion
  12.4 0.8 copy.12
  14.1 1.2 reduce-window.6
  16.2 11.8 %scatter_custom_fusion.1 = f32[96]{0:T(128)S(1)} fusion(s32[3072]{0:T(1024)S(1)} %bitcast.58, f32[3072]{0:T(1024)S(1)} %reshape.139, f32[]{:T(128)} %constant.16.clone.1), kind=kCustom, calls=%fused_computation.52 | custom fusion | bytes 388 | tf_op jit(solution)/shard_map/scatter | solution.py:32
  28.0 11.8 %scatter_custom_fusion = s32[96]{0:T(128)S(1)} fusion(s32[3072]{0:T(1024)S(1)} %bitcast.59, s32[3072]{0:T(1024)S(1)} %add_select_fusion, s32[]{:T(128)} %constant.17.clone.1), kind=kCustom, calls=%fused_computation.54 | custom fusion | bytes 388 | tf_op jit(solution)/shard_map/scatter | solution.py:29
  39.9 0.8 gather_fusion.1
  40.7 0.8 fusion.12
  41.5 3.5 %all-to-all-start.2 = ((bf16[4,24,896]{2,1,0:T(8,128)(2,1)}), bf16[4,24,896]{2,1,0:T(8,128)(2,1)S(1)}, u32[]{:S(2)}, u32[]{:S(2)}) async-start(bf16[4,24,896]{2,1,0:T(8,128)(2,1)} %fusion.12), calls=%async_computation.2 | async-start | bytes 344064 | tf_op jit(solution)/shard_map/all_to_all | solution.py:73
  45.0 1.5 gather_fusion
  46.5 3.5 %all-to-all-done.2 = bf16[4,24,896]{2,1,0:T(8,128)(2,1)S(1)} async-done(((bf16[4,24,896]{2,1,0:T(8,128)(2,1)}), bf16[4,24,896]{2,1,0:T(8,128)(2,1)S(1)}, u32[]{:S(2)}, u32[]{:S(2)}) %all-to-all-start.2) | async-done | bytes 172064 | tf_op jit(solution)/shard_map/all_to_all | solution.py:73
  50.0 3.4 %all-to-all-start = ((bf16[4,24,896]{2,1,0:T(8,128)(2,1)}), bf16[4,24,896]{2,1,0:T(8,128)(2,1)S(1)}, u32[]{:S(2)}, u32[]{:S(2)}) async-start(bf16[4,24,896]{2,1,0:T(8,128)(2,1)} %bitcast.3), calls=%async_computation | async-start | bytes 344064 | tf_op jit(solution)/shard_map/all_to_all | solution.py:48
  53.4 3.0 %fusion.13 = f32[96,1024]{1,0:T(8,128)} fusion(bf16[96,896]{1,0:T(8,128)(2,1)S(1)} %bitcast.52, bf16[512,896]{1,0:T(8,128)(2,1)} %collective-permute-done, bf16[512,896]{1,0:T(8,128)(2,1)S(1)} %bitcast.62, pred[]{:T(512)S(6)} %eq.36), kind=kOutput, calls=%fused_computation.28 | convolution fusion | flops 184418304 | bytes 2400257 | tf_op jit(solution)/shard_map/dot_general | solution.py:83
  56.4 1.9 %all-to-all-done = bf16[4,24,896]{2,1,0:T(8,128)(2,1)S(1)} async-done(((bf16[4,24,896]{2,1,0:T(8,128)(2,1)}), bf16[4,24,896]{2,1,0:T(8,128)(2,1)S(1)}, u32[]{:S(2)}, u32[]{:S(2)}) %all-to-all-start) | async-done | bytes 172064 | tf_op jit(solution)/shard_map/all_to_all | solution.py:48
  58.3 2.7 %fusion.2 = f32[96,1024]{1,0:T(8,128)} fusion(bf16[96,896]{1,0:T(8,128)(2,1)S(1)} %bitcast.50, bf16[1,896,1024]{2,1,0:T(8,128)(2,1)} %all-gather.3.cloned.1.call-done), kind=kOutput, calls=%fused_computation.9 | convolution fusion | flops 176160768 | bytes 2400256 | tf_op jit(solution)/shard_map/dot_general | solution.py:55
  61.1 43.3 %all-reduce.5.cloned.1.call-done = (f32[96,1024]{1,0:T(8,128)}, f32[96,1024]{1,0:T(8,128)}) async-done(((f32[96,1024]{1,0:T(8,128)}, f32[96,1024]{1,0:T(8,128)}), (f32[96,1024]{1,0:T(8,128)}, f32[96,1024]{1,0:T(8,128)})) %all-reduce.5.cloned.1.call-update) | async-done | bytes 786448 | tf_op jit(solution)/shard_map/psum | solution.py:55
  104.4 3.0 %convolution_convert_fusion = bf16[1024,896]{1,0:T(8,128)(2,1)} fusion(bf16[96,896]{1,0:T(8,128)(2,1)S(1)} %bitcast.53, f32[96,1024]{1,0:T(8,128)} %get-tuple-element.4), kind=kOutput, calls=%fused_computation.11 | convolution fusion | flops 177569792 | bytes 2400256 | tf_op jit(solution)/shard_map/dot_general | solution.py:99
  107.7 1.9 %convolution_convert_fusion.1 = bf16[896,1024]{1,0:T(8,128)(2,1)} fusion(bf16[96,896]{1,0:T(8,128)(2,1)S(1)} %bitcast.51, bf16[96,1024]{1,0:T(8,128)(2,1)S(1)} %multiply_convert_fusion), kind=kOutput, calls=%fused_computation.12 | convolution fusion | flops 177078272 | bytes 2203648 | tf_op jit(solution)/shard_map/dot_general | solution.py:98
  109.6 3.0 %convolution_convert_fusion.2 = bf16[96,896]{1,0:T(8,128)(2,1)} fusion(bf16[512,896]{1,0:T(8,128)(2,1)} %collective-permute-done, bf16[512,896]{1,0:T(8,128)(2,1)S(1)} %bitcast.63, pred[]{:T(512)S(6)} %eq.36, f32[96,1024]{1,0:T(8,128)S(1)} %copy-done.1), kind=kOutput, calls=%fused_computation.16 | convolution fusion | flops 184995840 | bytes 2400257 | tf_op jit(solution)/shard_map/dot_general | solution.py:57
  112.6 3.4 %all-to-all-start.1 = ((bf16[4,24,896]{2,1,0:T(8,128)(2,1)}), bf16[4,24,896]{2,1,0:T(8,128)(2,1)S(1)}, u32[]{:S(2)}, u32[]{:S(2)}) async-start(bf16[4,24,896]{2,1,0:T(8,128)(2,1)} %bitcast.7), calls=%async_computation.1 | async-start | bytes 344064 | tf_op jit(solution)/shard_map/all_to_all | solution.py:58
  116.0 1.3 fusion.4
  117.3 3.6 %all-to-all-done.1 = bf16[4,24,896]{2,1,0:T(8,128)(2,1)S(1)} async-done(((bf16[4,24,896]{2,1,0:T(8,128)(2,1)}), bf16[4,24,896]{2,1,0:T(8,128)(2,1)S(1)}, u32[]{:S(2)}, u32[]{:S(2)}) %all-to-all-start.1) | async-done | bytes 172064 | tf_op jit(solution)/shard_map/all_to_all | solution.py:58
  121.0 3.3 %all-to-all-start.3 = ((bf16[4,24,896]{2,1,0:T(8,128)(2,1)}), bf16[4,24,896]{2,1,0:T(8,128)(2,1)S(1)}, u32[]{:S(2)}, u32[]{:S(2)}) async-start(bf16[4,24,896]{2,1,0:T(8,128)(2,1)} %bitcast.11), calls=%async_computation.3 | async-start | bytes 344064 | tf_op jit(solution)/shard_map/all_to_all | solution.py:89
  124.3 1.8 %scatter_custom_fusion.2 = f32[385,896]{1,0:T(8,128)S(1)} fusion(s32[96]{0:T(128)S(1)} %compare_select_fusion.1, f32[]{:T(128)} %constant.16.clone.1, bf16[96,896]{1,0:T(8,128)(2,1)S(1)} %bitcast.54, f32[96]{0:T(128)S(1)} %scatter_custom_fusion.1), kind=kCustom, calls=%fused_computation.19 | custom fusion | flops 258048 | bytes 1552388 | tf_op jit(solution)/shard_map/scatter-add | solution.py:68
  126.1 0.9 slice.29
  127.0 2.3 %all-to-all-done.3 = bf16[4,24,896]{2,1,0:T(8,128)(2,1)S(1)} async-done(((bf16[4,24,896]{2,1,0:T(8,128)(2,1)}), bf16[4,24,896]{2,1,0:T(8,128)(2,1)S(1)}, u32[]{:S(2)}, u32[]{:S(2)}) %all-to-all-start.3) | async-done | bytes 172064 | tf_op jit(solution)/shard_map/all_to_all | solution.py:89
  129.3 1.7 scatter_custom_fusion.3
  131.0 0.9 slice.28
  132.0 3.9 %reduce-scatter.5.cloned.1.call-done = bf16[512,896]{1,0:T(8,128)(2,1)} async-done(((bf16[1024,896]{1,0:T(8,128)(2,1)}), bf16[512,896]{1,0:T(8,128)(2,1)}) %reduce-scatter.5.cloned.1.call-update) | async-done | bytes 917520 | tf_op jit(solution)/shard_map/reduce_scatter | solution.py:106
  135.8 31.7 %reduce-scatter.3.cloned.1.call-done = bf16[896,512]{1,0:T(8,128)(2,1)} async-done(((bf16[896,1024]{1,0:T(8,128)(2,1)}), bf16[896,512]{1,0:T(8,128)(2,1)}) %reduce-scatter.3.cloned.1.call-update) | async-done | bytes 917520 | tf_op jit(solution)/shard_map/reduce_scatter | solution.py:103
  (45 shorter events, 2.3 us)
Async XLA Ops:
  7.2 8.7 %copy-start.5 = (s32[384,8]{0,1:T(8,128)S(1)}, s32[384,8]{0,1:T(8,128)}, u32[]{:S(2)}) copy-start(s32[384,8]{0,1:T(8,128)} %param.8) | copy-start | bytes 36868
  7.2 32.6 %copy-start.2 = (bf16[384,896]{1,0:T(8,128)(2,1)S(1)}, bf16[384,896]{1,0:T(8,128)(2,1)}, u32[]{:S(2)}) copy-start(bf16[384,896]{1,0:T(8,128)(2,1)} %param.11) | copy-start | bytes 2064388
  7.2 51.1 %all-gather.3.cloned.1.call-start = ((), (), s32[]{:S(2)}) async-start(), calls=%async_computation.8 | async-start | bytes 2752512 | tf_op jit(solution)/shard_map/all_gather | solution.py:52
  7.9 45.5 %collective-permute-start = (bf16[512,896]{1,0:T(8,128)(2,1)}, bf16[512,896]{1,0:T(8,128)(2,1)}, u32[]{:S(2)}, u32[]{:S(2)}) collective-permute-start(bf16[512,896]{1,0:T(8,128)(2,1)} %bitcast.61), channel_id=1, source_target_pairs={{0,1},{1,0},{2,3},{3,2},{4,5},{5,4},{6,7},{7,6},{8,9},{9,8},{10,11... | collective-permute-start | bytes 2752520 | tf_op jit(solution)/shard_map/ppermute | solution.py:11
  16.1 28.8 %copy-start.3 = (bf16[384,896]{1,0:T(8,128)(2,1)S(1)}, bf16[384,896]{1,0:T(8,128)(2,1)}, u32[]{:S(2)}) copy-start(bf16[384,896]{1,0:T(8,128)(2,1)} %param.6) | copy-start | bytes 2064388
  41.5 11.9 %copy-start.6 = (bf16[1,512,896]{2,1,0:T(8,128)(2,1)S(1)}, bf16[1,512,896]{2,1,0:T(8,128)(2,1)}, u32[]{:S(2)}) copy-start(bf16[1,512,896]{2,1,0:T(8,128)(2,1)} %param.10) | copy-start | bytes 2752516
  41.5 8.5 %all-to-all-start.2 = ((bf16[4,24,896]{2,1,0:T(8,128)(2,1)}), bf16[4,24,896]{2,1,0:T(8,128)(2,1)S(1)}, u32[]{:S(2)}, u32[]{:S(2)}) async-start(bf16[4,24,896]{2,1,0:T(8,128)(2,1)} %fusion.12), calls=%async_computation.2 | async-start | bytes 344064 | tf_op jit(solution)/shard_map/all_to_all | solution.py:73
  50.0 8.4 %all-to-all-start = ((bf16[4,24,896]{2,1,0:T(8,128)(2,1)}), bf16[4,24,896]{2,1,0:T(8,128)(2,1)S(1)}, u32[]{:S(2)}, u32[]{:S(2)}) async-start(bf16[4,24,896]{2,1,0:T(8,128)(2,1)} %bitcast.3), calls=%async_computation | async-start | bytes 344064 | tf_op jit(solution)/shard_map/all_to_all | solution.py:48
  53.3 51.1 %all-reduce.5.cloned.1.call-start = ((), (), s32[]{:S(2)}) async-start(), calls=%async_computation.9 | async-start | bytes 1572864 | tf_op jit(solution)/shard_map/psum | solution.py:55
  61.1 74.8 %reduce-scatter.5.cloned.1.call-start = ((), (), s32[]{:S(2)}) async-start(), calls=%async_computation.7 | async-start | bytes 2752512 | tf_op jit(solution)/shard_map/reduce_scatter | solution.py:106
  104.4 3.1 %copy-start.1 = (f32[96,1024]{1,0:T(8,128)S(1)}, f32[96,1024]{1,0:T(8,128)}, u32[]{:S(2)}) copy-start(f32[96,1024]{1,0:T(8,128)} %get-tuple-element.4) | copy-start | bytes 1179652
  104.4 3.1 %copy-start.4 = (f32[96,1024]{1,0:T(8,128)S(1)}, f32[96,1024]{1,0:T(8,128)}, u32[]{:S(2)}) copy-start(f32[96,1024]{1,0:T(8,128)} %get-tuple-element.5) | copy-start | bytes 1179652
  107.5 60.1 %reduce-scatter.3.cloned.1.call-start = ((), (), s32[]{:S(2)}) async-start(), calls=%async_computation.6 | async-start | bytes 2752512 | tf_op jit(solution)/shard_map/reduce_scatter | solution.py:103
  109.6 6.3 %copy-start = (bf16[1,896,1024]{2,1,0:T(8,128)(2,1)S(1)}, bf16[1,896,1024]{2,1,0:T(8,128)(2,1)}, u32[]{:S(2)}) copy-start(bf16[1,896,1024]{2,1,0:T(8,128)(2,1)} %all-gather.3.cloned.1.call-done) | copy-start | bytes 5505028
  112.6 8.4 %all-to-all-start.1 = ((bf16[4,24,896]{2,1,0:T(8,128)(2,1)}), bf16[4,24,896]{2,1,0:T(8,128)(2,1)S(1)}, u32[]{:S(2)}, u32[]{:S(2)}) async-start(bf16[4,24,896]{2,1,0:T(8,128)(2,1)} %bitcast.7), calls=%async_computation.1 | async-start | bytes 344064 | tf_op jit(solution)/shard_map/all_to_all | solution.py:58
  121.0 8.4 %all-to-all-start.3 = ((bf16[4,24,896]{2,1,0:T(8,128)(2,1)}), bf16[4,24,896]{2,1,0:T(8,128)(2,1)S(1)}, u32[]{:S(2)}, u32[]{:S(2)}) async-start(bf16[4,24,896]{2,1,0:T(8,128)(2,1)} %bitcast.11), calls=%async_computation.3 | async-start | bytes 344064 | tf_op jit(solution)/shard_map/all_to_all | solution.py:89
Sparse Core Ops, SparseCore 0:
  9.5 41.8 all-gather.2
  61.2 43.2 all-reduce.4
  107.6 28.2 reduce-scatter.4
  138.5 29.0 reduce-scatter.2
